TPU v7x, 256 devices: a whole 4x4x8 slice. The times are simulated.
256 devices in a mesh: px: 16 (over y, x), py: 16 (over z, core).
Axes of the slice: x: 4, y: 4, z: 8, core: 2. Of those that a mesh axis runs over, the one named last changes fastest.
Arguments:
- start_field: float32 [128, 256, 512], P('px', 'py'), may hold values from -1.7 to 1.7
- known: float32 [8, 128, 256, 512], P(None, 'px', 'py'), may hold values from -1 to 1
Outputs:
- solution_field: float32 [128, 256, 512], P('px', 'py')
- residual: float32 [128, 256, 512], P('px', 'py')
All inputs are finite; a program needn't handle non-finite values.
Results may differ from a plain program's by a relative error of at most 0.01.
Values sent between devices are 32-bit elements; how exact they have to be, the bound alone decides.
No kernel may reach another device: no remote copies, remote signals or barrier semaphores. Data moves between devices by JAX's collectives and lax.ppermute only.
A program may use at most 64 MiB of HBM per device.

v0:
```python
import jax
import jax.numpy as jnp
from jax import lax
from jax.sharding import PartitionSpec as P

NEWTON = 2
ITERS = 3
DIFFUSION = 0.5
SHIFT = 4.0
EPS = 1e-06


def extended(cells, sides, width):
    for axis, dim in sides:
        count = lax.axis_size(axis)
        ends = count - 1
        head = lax.slice_in_dim(cells, 0, width, axis=dim)
        tail = lax.slice_in_dim(cells, cells.shape[dim] - width, cells.shape[dim], axis=dim)
        cells = jnp.concatenate(
            [
                lax.ppermute(tail, axis, [(i, (i + 1) % count) for i in range(ends)]),
                cells,
                lax.ppermute(head, axis, [((i + 1) % count, i) for i in range(ends)]),
            ],
            axis=dim,
        )
    return cells


def laplace(field):
    padded = extended(field, (("px", 0), ("py", 1)), 1)
    zero = jnp.zeros_like(field[:, :, :1])
    upper = jnp.concatenate([field[:, :, 1:], zero], axis=2)
    lower = jnp.concatenate([zero, field[:, :, :-1]], axis=2)
    beside = padded[2:, 1:-1, :] + padded[:-2, 1:-1, :]
    beside = beside + padded[1:-1, 2:, :] + padded[1:-1, :-2, :]
    return beside + upper + lower - 6.0 * field


def allen_cahn(field, lap):
    return DIFFUSION * lap + field - field * field * field


def solve_small(hess, beta):
    normal = jnp.sum(hess[:, :, None] * hess[:, None, :], axis=0)
    target = beta * hess[0]
    lower = jnp.linalg.cholesky(normal)
    count = normal.shape[0]
    forward = []
    for i in range(count):
        acc = target[i]
        for j in range(i):
            acc = acc - lower[i, j] * forward[j]
        forward.append(acc / lower[i, i])
    back = [None] * count
    for i in reversed(range(count)):
        acc = forward[i]
        for j in range(i + 1, count):
            acc = acc - lower[j, i] * back[j]
        back[i] = acc / lower[i, i]
    return jnp.stack(back)


def local(start_field, known):
    cells = float(
        start_field.shape[0]
        * lax.axis_size("px")
        * start_field.shape[1]
        * lax.axis_size("py")
        * start_field.shape[2]
    )
    field = start_field
    lap_field = laplace(field)
    for step in range(NEWTON):
        force = allen_cahn(field, lap_field)
        diffs = field[None] - known
        dist_local = jnp.sum(diffs * diffs, axis=(1, 2, 3))
        first_sum, force_sq = lax.psum((dist_local, jnp.sum(force * force)), ("px", "py"))
        beta = jnp.sqrt(force_sq + EPS)
        basis = [-force / beta]
        lap_basis = []
        jac_diag = 1.0 - 3.0 * field * field
        hess = jnp.zeros((ITERS + 1, ITERS), jnp.float32)
        for k in range(ITERS):
            lap_vec = laplace(basis[k])
            lap_basis.append(lap_vec)
            image = DIFFUSION * lap_vec + jac_diag * basis[k]
            heights_local = jnp.stack([jnp.sum(vec * image) for vec in basis])
            summed = lax.psum(heights_local, ("px", "py"))
            rest = image
            for j in range(k + 1):
                rest = rest - summed[j] * basis[j]
            height = jnp.sqrt(lax.psum(jnp.sum(rest * rest), ("px", "py")) + EPS)
            hess = hess.at[: k + 1, k].set(summed).at[k + 1, k].set(height)
            if k < ITERS - 1:
                basis.append(rest / height)
        coeffs = solve_small(hess, beta)
        delta = coeffs[0] * basis[0]
        for j in range(1, ITERS):
            delta = delta + coeffs[j] * basis[j]
        inner = lax.psum(jnp.sum(diffs * delta[None], axis=(1, 2, 3)), ("px", "py"))
        mean_dist = first_sum / cells + EPS
        weight = 1.0 / mean_dist + SHIFT
        total = jnp.sum(2.0 * inner / (cells * mean_dist * mean_dist * weight))
        scale = 1.0 / (1.0 + jnp.abs(total))
        field = field + scale * delta
        lap_field = laplace(field)
    return (field, allen_cahn(field, lap_field))


def solution(mesh):
    placed = (P("px", "py", None), P(None, "px", "py", None))
    return jax.shard_map(
        local,
        mesh=mesh,
        in_specs=placed,
        out_specs=(P("px", "py", None), P("px", "py", None)),
        check_vma=False,
    )
```

profile of v0, /device:TPU:38, one launch (start us, length us, event | category | flops | bytes accessed | tf_op | source)
XLA Modules:
  0.0 1435.6 jit_solution(6165251050151356504)
XLA Ops:
  1.5 2.7 collective-permute-start
  4.2 5.2 collective-permute-start.1
  19.9 80.0 %psum.126 = f32[]{:T(128)} all-reduce(f32[]{:T(128)} %get-tuple-element.179), channel_id=1, replica_groups=mesh['px'=16,'py'=16] {'px','py'}, use_global_device_ids=true, to_apply=%region_1.0 | all-reduce | flops 1 | bytes 8 | tf_op jit(solution)/shard_map/psum | solution.py:78
  100.6 3.4 collective-permute-start.5
  104.0 2.5 collective-permute-start.4
  107.2 4.7 collective-permute-done.4
  116.5 2.5 collective-permute-done.7
  119.8 73.3 %psum.127 = f32[1]{0:T(128)} all-reduce(f32[1]{0:T(128)} %bitcast), channel_id=1, replica_groups=mesh['px'=16,'py'=16] {'px','py'}, use_global_device_ids=true, to_apply=%region_3.0 | all-reduce | flops 1 | bytes 8 | tf_op jit(solution)/shard_map/psum | solution.py:89
  194.5 74.3 %psum.128 = f32[]{:T(128)} all-reduce(f32[]{:T(128)} %multiply_reduce_fusion.21), channel_id=1, replica_groups=mesh['px'=16,'py'=16] {'px','py'}, use_global_device_ids=true, to_apply=%region_5.0 | all-reduce | flops 1 | bytes 8 | tf_op jit(solution)/shard_map/psum | solution.py:93
  270.2 3.4 collective-permute-start.9
  273.6 2.5 collective-permute-start.8
  277.3 4.1 collective-permute-done.8
  291.0 73.4 %psum.129 = f32[2]{0:T(128)S(1)} all-reduce(f32[2]{0:T(128)S(1)} %pad_maximum_fusion.92), channel_id=1, replica_groups=mesh['px'=16,'py'=16] {'px','py'}, use_global_device_ids=true, to_apply=%region_9.0 | all-reduce | flops 2 | bytes 16 | tf_op jit(solution)/shard_map/psum | solution.py:89
  367.1 74.1 %psum.130 = f32[]{:T(128)} all-reduce(f32[]{:T(128)} %get-tuple-element.174), channel_id=1, replica_groups=mesh['px'=16,'py'=16] {'px','py'}, use_global_device_ids=true, to_apply=%region_11.0 | all-reduce | flops 1 | bytes 8 | tf_op jit(solution)/shard_map/psum | solution.py:93
  441.9 3.4 collective-permute-start.13
  448.6 4.6 collective-permute-done.12
  461.1 2.8 multiply_reduce_fusion.17
  466.0 75.2 %psum.131 = f32[3]{0:T(128)S(1)} all-reduce(f32[3]{0:T(128)S(1)} %pad_maximum_fusion.93), channel_id=1, replica_groups=mesh['px'=16,'py'=16] {'px','py'}, use_global_device_ids=true, to_apply=%region_16.0 | all-reduce | flops 3 | bytes 24 | tf_op jit(solution)/shard_map/psum | solution.py:89
  543.7 3.6 multiply_reduce_fusion.14
  548.8 74.0 %psum.132 = f32[]{:T(128)} all-reduce(f32[]{:T(128)} %multiply_reduce_fusion.14), channel_id=1, replica_groups=mesh['px'=16,'py'=16] {'px','py'}, use_global_device_ids=true, to_apply=%region_18.0 | all-reduce | flops 1 | bytes 8 | tf_op jit(solution)/shard_map/psum | solution.py:93
  636.7 73.7 %all-reduce.21 = (f32[8]{0:T(128)S(1)}, f32[8]{0:T(128)S(1)}) all-reduce(f32[8]{0:T(128)S(1)} %get-tuple-element.150, f32[8]{0:T(128)S(1)} %get-tuple-element.149), channel_id=1, replica_groups=mesh['px'=16,'py'=16] {'px','py'}, use_global_device_ids=true, to_apply=%region_25.27 | all-reduce | flops 16 | bytes 128 | tf_op jit(solution)/shard_map/psum | solution.py:78
  711.9 3.3 collective-permute-start.17
  715.2 2.5 collective-permute-start.16
  717.7 5.4 collective-permute-done.16
  727.6 2.5 collective-permute-done.19
  731.0 73.4 %psum.135 = f32[]{:T(128)} all-reduce(f32[]{:T(128)} %get-tuple-element.171), channel_id=1, replica_groups=mesh['px'=16,'py'=16] {'px','py'}, use_global_device_ids=true, to_apply=%region_28.0 | all-reduce | flops 1 | bytes 8 | tf_op jit(solution)/shard_map/psum | solution.py:78
  805.1 3.4 collective-permute-start.21
  808.5 2.5 collective-permute-start.20
  811.0 5.4 collective-permute-done.20
  820.9 2.5 collective-permute-done.23
  824.3 73.4 %psum.136 = f32[1]{0:T(128)} all-reduce(f32[1]{0:T(128)} %bitcast.32), channel_id=1, replica_groups=mesh['px'=16,'py'=16] {'px','py'}, use_global_device_ids=true, to_apply=%region_30.0 | all-reduce | flops 1 | bytes 8 | tf_op jit(solution)/shard_map/psum | solution.py:89
  899.0 74.1 %psum.137 = f32[]{:T(128)} all-reduce(f32[]{:T(128)} %multiply_reduce_fusion.11), channel_id=1, replica_groups=mesh['px'=16,'py'=16] {'px','py'}, use_global_device_ids=true, to_apply=%region_32.0 | all-reduce | flops 1 | bytes 8 | tf_op jit(solution)/shard_map/psum | solution.py:93
  974.5 3.4 collective-permute-start.25
  977.9 2.5 collective-permute-start.24
  980.4 5.4 collective-permute-done.24
  995.3 73.4 %psum.138 = f32[2]{0:T(128)S(1)} all-reduce(f32[2]{0:T(128)S(1)} %pad_maximum_fusion.94), channel_id=1, replica_groups=mesh['px'=16,'py'=16] {'px','py'}, use_global_device_ids=true, to_apply=%region_35.0 | all-reduce | flops 2 | bytes 16 | tf_op jit(solution)/shard_map/psum | solution.py:89
  1071.4 74.0 %psum.139 = f32[]{:T(128)} all-reduce(f32[]{:T(128)} %get-tuple-element.166), channel_id=1, replica_groups=mesh['px'=16,'py'=16] {'px','py'}, use_global_device_ids=true, to_apply=%region_37.0 | all-reduce | flops 1 | bytes 8 | tf_op jit(solution)/shard_map/psum | solution.py:93
  1146.1 3.4 collective-permute-start.29
  1152.9 4.6 collective-permute-done.28
  1166.0 2.7 multiply_reduce_fusion.7
  1170.8 75.2 %psum.140 = f32[3]{0:T(128)S(1)} all-reduce(f32[3]{0:T(128)S(1)} %pad_maximum_fusion.95), channel_id=1, replica_groups=mesh['px'=16,'py'=16] {'px','py'}, use_global_device_ids=true, to_apply=%region_41.0 | all-reduce | flops 3 | bytes 24 | tf_op jit(solution)/shard_map/psum | solution.py:89
  1248.5 3.6 multiply_reduce_fusion.4
  1253.5 74.1 %psum.141 = f32[]{:T(128)} all-reduce(f32[]{:T(128)} %multiply_reduce_fusion.4), channel_id=1, replica_groups=mesh['px'=16,'py'=16] {'px','py'}, use_global_device_ids=true, to_apply=%region_43.0 | all-reduce | flops 1 | bytes 8 | tf_op jit(solution)/shard_map/psum | solution.py:93
  1341.6 73.5 %all-reduce.20 = (f32[8]{0:T(128)S(1)}, f32[8]{0:T(128)S(1)}) all-reduce(f32[8]{0:T(128)S(1)} %get-tuple-element.148, f32[8]{0:T(128)S(1)} %get-tuple-element.147), channel_id=1, replica_groups=mesh['px'=16,'py'=16] {'px','py'}, use_global_device_ids=true, to_apply=%region_48.0 | all-reduce | flops 16 | bytes 128 | tf_op jit(solution)/shard_map/psum | solution.py:78
  1416.4 3.3 collective-permute-start.33
  1419.8 2.5 collective-permute-start.32
  1422.3 5.4 collective-permute-done.32
  1432.2 2.5 collective-permute-done.35
  (157 shorter events, 107.0 us)
Async XLA Ops:
  0.6 18.4 %copy-start = (f32[8,16,512]{2,1,0:T(8,128)S(1)}, f32[8,16,512]{2,1,0:T(8,128)}, u32[]{:S(2)}) copy-start(f32[8,16,512]{2,1,0:T(8,128)} %param.27) | copy-start | bytes 786436
  1.5 10.5 collective-permute-start
  4.2 6.8 collective-permute-start.1
  12.0 5.6 collective-permute-start.2
  14.0 5.1 collective-permute-start.3
  100.6 6.5 collective-permute-start.5
  104.0 7.9 collective-permute-start.4
  112.0 4.5 collective-permute-start.6
  113.9 5.1 collective-permute-start.7
  270.2 7.1 collective-permute-start.9
  273.6 7.9 collective-permute-start.8
  281.5 5.1 collective-permute-start.10
  283.4 5.1 collective-permute-start.11
  441.9 6.7 collective-permute-start.13
  445.3 7.9 collective-permute-start.12
  453.2 7.9 collective-permute-start.14
  455.1 6.0 collective-permute-start.15
  461.1 175.0 %copy-start.1 = (f32[8,8,16,512]{3,2,1,0:T(8,128)S(1)}, f32[8,8,16,512]{3,2,1,0:T(8,128)}, u32[]{:S(2)}) copy-start(f32[8,8,16,512]{3,2,1,0:T(8,128)} %param.28) | copy-start | bytes 6291460
  711.9 5.9 collective-permute-start.17
  715.2 7.9 collective-permute-start.16
  723.1 4.5 collective-permute-start.18
  725.0 5.1 collective-permute-start.19
  805.1 5.9 collective-permute-start.21
  808.5 7.9 collective-permute-start.20
  816.4 4.5 collective-permute-start.22
  818.3 5.1 collective-permute-start.23
  974.5 5.9 collective-permute-start.25
  977.9 7.9 collective-permute-start.24
  985.8 5.1 collective-permute-start.26
  987.8 5.1 collective-permute-start.27
  1146.1 6.7 collective-permute-start.29
  1149.5 7.9 collective-permute-start.28
  1158.1 7.9 collective-permute-start.30
  1160.0 6.0 collective-permute-start.31
  1416.4 19.2 %copy-start.2 = (f32[8,16,512]{2,1,0:T(8,128)}, f32[8,16,512]{2,1,0:T(8,128)S(1)}, u32[]{:S(2)}) copy-start(f32[8,16,512]{2,1,0:T(8,128)S(1)} %multiply_add_fusion) | copy-start | bytes 786436
  1416.4 5.9 collective-permute-start.33
  1419.8 7.9 collective-permute-start.32
  1427.7 4.5 collective-permute-start.34
  1429.6 5.1 collective-permute-start.35
where the time goes:
time: 1440 us
  blocking collectives  1190 us (83%)
  starting transfers between devices  93.6 us (6%)
  waiting for transfers between devices  55.3 us (4%)
  other arithmetic  50.1 us (3%)
  between operations  27.2 us (2%)
  local copies, waits for them, and re-layouts  20.1 us (1%)
    psum x6, blocking collectives, local(): height = jnp.sqrt(lax.psum(jnp.sum(rest * rest), ('px', 'py')) + EPS)  445 us
    psum x6, blocking collectives, local(): summed = lax.psum(heights_local, ('px', 'py'))  444 us
    psum x4, blocking collectives, local(): lax.psum((dist_local, jnp.sum(force * force)), ('px', 'py'))  301 us
    ppermute x18, starting transfers between devices, extended(): lax.ppermute(tail, axis, [(i, (i + 1) % count) for i in range(ends)])  53.6 us
    ppermute x18, starting transfers between devices, extended(): lax.ppermute(head, axis, [((i + 1) % count, i) for i in range(ends)])  40 us
    ppermute x18, waiting for transfers between devices, extended(): lax.ppermute(head, axis, [((i + 1) % count, i) for i in range(ends)])  39.6 us
  transfers between devices with their start and end apart: 36, of which 16 were waited for; matrix products, arithmetic and copies ran while one was open for 1% of the time, Pallas kernels for 0%

commit v1 on v0

--- a/solution.py
+++ b/solution.py
@@ -86,7 +86,7 @@
             lap_basis.append(lap_vec)
             image = DIFFUSION * lap_vec + jac_diag * basis[k]
             heights_local = jnp.stack([jnp.sum(vec * image) for vec in basis])
-            summed = lax.psum(heights_local, ("px", "py"))
+            summed = lax.psum(lax.psum(heights_local, "px"), "py")
             rest = image
             for j in range(k + 1):
                 rest = rest - summed[j] * basis[j]

time: 1440 us -> 1340 us (0.931)
  blocking collectives: 1190 us -> 1090 us
    psum x6 -> x12, blocking collectives: 444 us -> 303 us  [local(): summed = lax.psum(lax.psum(heights_local, 'px'), 'py')]
    psum x6, blocking collectives: 445 us -> 488 us  [local(): height = jnp.sqrt(lax.psum(jnp.sum(rest * rest), ('px', 'py')) + EPS)]
  transfers between devices with their start and end apart: 36 -> 36, of which waited for: 16 -> 18; matrix products, arithmetic and copies ran while one was open for 1% -> 1% of each run, Pallas kernels for 0% -> 0%
where the time goes in v1:
time: 1340 us; the launch traced here: 1330 us
  blocking collectives  1090 us (81%)
  starting transfers between devices  91.7 us (7%)
  waiting for transfers between devices  64.7 us (5%)
  other arithmetic  42.9 us (3%)
  between operations  27.6 us (2%)
  local copies, waits for them, and re-layouts  18.4 us (1%)
    psum x6, blocking collectives, local(): height = jnp.sqrt(lax.psum(jnp.sum(rest * rest), ('px', 'py')) + EPS)  488 us
    psum x12, blocking collectives, local(): summed = lax.psum(lax.psum(heights_local, 'px'), 'py')  303 us
    psum x4, blocking collectives, local(): lax.psum((dist_local, jnp.sum(force * force)), ('px', 'py'))  297 us
    ppermute x18, starting transfers between devices, extended(): lax.ppermute(tail, axis, [(i, (i + 1) % count) for i in range(ends)])  51.6 us
    ppermute x18, waiting for transfers between devices, extended(): lax.ppermute(head, axis, [((i + 1) % count, i) for i in range(ends)])  45.5 us
    ppermute x18, starting transfers between devices, extended(): lax.ppermute(head, axis, [((i + 1) % count, i) for i in range(ends)])  40.1 us
  transfers between devices with their start and end apart: 36, of which 18 were waited for; matrix products, arithmetic and copies ran while one was open for 1% of the time, Pallas kernels for 0%

profile of v1, /device:TPU:38, one launch (start us, length us, event | category | flops | bytes accessed | tf_op | source)
XLA Modules:
  0.0 1333.5 jit_solution(14833187763406653205)
XLA Ops:
  1.5 3.4 collective-permute-start.1
  8.3 4.5 collective-permute-done
  20.7 76.6 %psum.168 = f32[]{:T(128)} all-reduce(f32[]{:T(128)} %get-tuple-element.179), channel_id=1, replica_groups=mesh['px'=16,'py'=16] {'px','py'}, use_global_device_ids=true, to_apply=%region_1.0 | all-reduce | flops 1 | bytes 8 | tf_op jit(solution)/shard_map/psum | solution.py:78
  98.1 3.4 collective-permute-start.5
  104.6 4.7 collective-permute-done.4
  113.9 2.5 collective-permute-done.7
  117.2 31.0 %psum.169 = f32[1]{0:T(128)} all-reduce(f32[1]{0:T(128)} %bitcast), channel_id=1, replica_groups=mesh['px'=16,'py'=16] {'px'}, use_global_device_ids=true, to_apply=%region_3.0 | all-reduce | flops 1 | bytes 8 | tf_op jit(solution)/shard_map/psum | solution.py:89
  148.9 19.9 %psum.170 = f32[1]{0:T(128)} all-reduce(f32[1]{0:T(128)} %psum.169), channel_id=1, replica_groups=mesh['px'=16,'py'=16] {'py'}, use_global_device_ids=true, to_apply=%region_4.0 | all-reduce | flops 1 | bytes 8 | tf_op jit(solution)/shard_map/psum | solution.py:89
  170.1 81.5 %psum.171 = f32[]{:T(128)} all-reduce(f32[]{:T(128)} %multiply_reduce_fusion.21), channel_id=1, replica_groups=mesh['px'=16,'py'=16] {'px','py'}, use_global_device_ids=true, to_apply=%region_6.0 | all-reduce | flops 1 | bytes 8 | tf_op jit(solution)/shard_map/psum | solution.py:93
  253.1 3.4 collective-permute-start.9
  260.2 4.1 collective-permute-done.8
  274.3 30.4 %psum.172 = f32[2]{0:T(128)S(1)} all-reduce(f32[2]{0:T(128)S(1)} %pad_maximum_fusion.92), channel_id=1, replica_groups=mesh['px'=16,'py'=16] {'px'}, use_global_device_ids=true, to_apply=%region_10.0 | all-reduce | flops 2 | bytes 16 | tf_op jit(solution)/shard_map/psum | solution.py:89
  304.8 20.0 %psum.173 = f32[2]{0:T(128)S(1)} all-reduce(f32[2]{0:T(128)S(1)} %psum.172), channel_id=1, replica_groups=mesh['px'=16,'py'=16] {'py'}, use_global_device_ids=true, to_apply=%region_11.0 | all-reduce | flops 2 | bytes 16 | tf_op jit(solution)/shard_map/psum | solution.py:89
  327.3 81.1 %psum.174 = f32[]{:T(128)} all-reduce(f32[]{:T(128)} %get-tuple-element.174), channel_id=1, replica_groups=mesh['px'=16,'py'=16] {'px','py'}, use_global_device_ids=true, to_apply=%region_13.0 | all-reduce | flops 1 | bytes 8 | tf_op jit(solution)/shard_map/psum | solution.py:93
  409.2 3.4 collective-permute-start.13
  415.2 5.3 collective-permute-done.12
  431.9 30.4 %psum.175 = f32[3]{0:T(128)S(1)} all-reduce(f32[3]{0:T(128)S(1)} %pad_maximum_fusion.93), channel_id=1, replica_groups=mesh['px'=16,'py'=16] {'px'}, use_global_device_ids=true, to_apply=%region_18.0 | all-reduce | flops 3 | bytes 24 | tf_op jit(solution)/shard_map/psum | solution.py:89
  462.3 20.0 %psum.176 = f32[3]{0:T(128)S(1)} all-reduce(f32[3]{0:T(128)S(1)} %psum.175), channel_id=1, replica_groups=mesh['px'=16,'py'=16] {'py'}, use_global_device_ids=true, to_apply=%region_19.0 | all-reduce | flops 3 | bytes 24 | tf_op jit(solution)/shard_map/psum | solution.py:89
  484.9 2.6 multiply_reduce_fusion.14
  489.0 81.1 %psum.177 = f32[]{:T(128)} all-reduce(f32[]{:T(128)} %multiply_reduce_fusion.14), channel_id=1, replica_groups=mesh['px'=16,'py'=16] {'px','py'}, use_global_device_ids=true, to_apply=%region_21.0 | all-reduce | flops 1 | bytes 8 | tf_op jit(solution)/shard_map/psum | solution.py:93
  584.3 73.4 %all-reduce.21 = (f32[8]{0:T(128)S(1)}, f32[8]{0:T(128)S(1)}) all-reduce(f32[8]{0:T(128)S(1)} %get-tuple-element.150, f32[8]{0:T(128)S(1)} %get-tuple-element.149), channel_id=1, replica_groups=mesh['px'=16,'py'=16] {'px','py'}, use_global_device_ids=true, to_apply=%region_28.30 | all-reduce | flops 16 | bytes 128 | tf_op jit(solution)/shard_map/psum | solution.py:78
  659.0 3.3 collective-permute-start.17
  662.3 2.5 collective-permute-start.16
  664.9 5.4 collective-permute-done.16
  674.8 3.0 collective-permute-done.19
  678.6 73.7 %psum.180 = f32[]{:T(128)} all-reduce(f32[]{:T(128)} %get-tuple-element.171), channel_id=1, replica_groups=mesh['px'=16,'py'=16] {'px','py'}, use_global_device_ids=true, to_apply=%region_31.0 | all-reduce | flops 1 | bytes 8 | tf_op jit(solution)/shard_map/psum | solution.py:78
  753.0 3.4 collective-permute-start.21
  758.9 5.4 collective-permute-done.20
  772.4 31.0 %psum.181 = f32[1]{0:T(128)} all-reduce(f32[1]{0:T(128)} %bitcast.32), channel_id=1, replica_groups=mesh['px'=16,'py'=16] {'px'}, use_global_device_ids=true, to_apply=%region_33.0 | all-reduce | flops 1 | bytes 8 | tf_op jit(solution)/shard_map/psum | solution.py:89
  803.3 20.2 %psum.182 = f32[1]{0:T(128)} all-reduce(f32[1]{0:T(128)} %psum.181), channel_id=1, replica_groups=mesh['px'=16,'py'=16] {'py'}, use_global_device_ids=true, to_apply=%region_34.0 | all-reduce | flops 1 | bytes 8 | tf_op jit(solution)/shard_map/psum | solution.py:89
  824.8 81.7 %psum.183 = f32[]{:T(128)} all-reduce(f32[]{:T(128)} %multiply_reduce_fusion.11), channel_id=1, replica_groups=mesh['px'=16,'py'=16] {'px','py'}, use_global_device_ids=true, to_apply=%region_36.0 | all-reduce | flops 1 | bytes 8 | tf_op jit(solution)/shard_map/psum | solution.py:93
  907.9 3.4 collective-permute-start.25
  913.8 5.4 collective-permute-done.24
  923.7 2.5 collective-permute-done.27
  929.2 30.4 %psum.184 = f32[2]{0:T(128)S(1)} all-reduce(f32[2]{0:T(128)S(1)} %pad_maximum_fusion.94), channel_id=1, replica_groups=mesh['px'=16,'py'=16] {'px'}, use_global_device_ids=true, to_apply=%region_39.0 | all-reduce | flops 2 | bytes 16 | tf_op jit(solution)/shard_map/psum | solution.py:89
  959.7 20.0 %psum.185 = f32[2]{0:T(128)S(1)} all-reduce(f32[2]{0:T(128)S(1)} %psum.184), channel_id=1, replica_groups=mesh['px'=16,'py'=16] {'py'}, use_global_device_ids=true, to_apply=%region_40.0 | all-reduce | flops 2 | bytes 16 | tf_op jit(solution)/shard_map/psum | solution.py:89
  982.2 81.1 %psum.186 = f32[]{:T(128)} all-reduce(f32[]{:T(128)} %get-tuple-element.166), channel_id=1, replica_groups=mesh['px'=16,'py'=16] {'px','py'}, use_global_device_ids=true, to_apply=%region_42.0 | all-reduce | flops 1 | bytes 8 | tf_op jit(solution)/shard_map/psum | solution.py:93
  1064.0 3.4 collective-permute-start.29
  1070.0 5.3 collective-permute-done.28
  1086.6 30.4 %psum.187 = f32[3]{0:T(128)S(1)} all-reduce(f32[3]{0:T(128)S(1)} %pad_maximum_fusion.95), channel_id=1, replica_groups=mesh['px'=16,'py'=16] {'px'}, use_global_device_ids=true, to_apply=%region_46.0 | all-reduce | flops 3 | bytes 24 | tf_op jit(solution)/shard_map/psum | solution.py:89
  1117.1 20.0 %psum.188 = f32[3]{0:T(128)S(1)} all-reduce(f32[3]{0:T(128)S(1)} %psum.187), channel_id=1, replica_groups=mesh['px'=16,'py'=16] {'py'}, use_global_device_ids=true, to_apply=%region_47.0 | all-reduce | flops 3 | bytes 24 | tf_op jit(solution)/shard_map/psum | solution.py:89
  1139.7 2.6 multiply_reduce_fusion.4
  1143.7 81.1 %psum.189 = f32[]{:T(128)} all-reduce(f32[]{:T(128)} %multiply_reduce_fusion.4), channel_id=1, replica_groups=mesh['px'=16,'py'=16] {'px','py'}, use_global_device_ids=true, to_apply=%region_49.0 | all-reduce | flops 1 | bytes 8 | tf_op jit(solution)/shard_map/psum | solution.py:93
  1239.0 73.4 %all-reduce.20 = (f32[8]{0:T(128)S(1)}, f32[8]{0:T(128)S(1)}) all-reduce(f32[8]{0:T(128)S(1)} %get-tuple-element.148, f32[8]{0:T(128)S(1)} %get-tuple-element.147), channel_id=1, replica_groups=mesh['px'=16,'py'=16] {'px','py'}, use_global_device_ids=true, to_apply=%region_54.0 | all-reduce | flops 16 | bytes 128 | tf_op jit(solution)/shard_map/psum | solution.py:78
  1313.8 3.3 collective-permute-start.33
  1317.1 2.5 collective-permute-start.32
  1319.7 5.4 collective-permute-done.32
  1329.6 3.0 collective-permute-done.35
  (165 shorter events, 120.7 us)
Async XLA Ops:
  0.6 103.3 %copy-start.3 = (s32[2]{0:T(128)S(1)}, s32[2]{0:T(128)}, u32[]{:S(2)}) copy-start(s32[2]{0:T(128)} %constant.311.clone.1) | copy-start | bytes 28
  0.6 19.2 %copy-start = (f32[8,16,512]{2,1,0:T(8,128)S(1)}, f32[8,16,512]{2,1,0:T(8,128)}, u32[]{:S(2)}) copy-start(f32[8,16,512]{2,1,0:T(8,128)} %param.27) | copy-start | bytes 786436
  1.5 5.8 collective-permute-start.1
  4.9 7.9 collective-permute-start
  12.8 5.5 collective-permute-start.2
  14.8 5.1 collective-permute-start.3
  98.1 6.5 collective-permute-start.5
  101.4 7.9 collective-permute-start.4
  109.4 4.5 collective-permute-start.6
  111.3 5.1 collective-permute-start.7
  253.1 7.2 collective-permute-start.9
  256.4 7.9 collective-permute-start.8
  264.4 4.5 collective-permute-start.10
  266.3 5.1 collective-permute-start.11
  409.2 6.0 collective-permute-start.13
  412.5 7.9 collective-permute-start.12
  420.5 6.3 collective-permute-start.14
  422.4 5.1 collective-permute-start.15
  427.5 156.1 %copy-start.1 = (f32[8,8,16,512]{3,2,1,0:T(8,128)S(1)}, f32[8,8,16,512]{3,2,1,0:T(8,128)}, u32[]{:S(2)}) copy-start(f32[8,8,16,512]{3,2,1,0:T(8,128)} %param.28) | copy-start | bytes 6291460
  659.0 5.9 collective-permute-start.17
  662.3 7.9 collective-permute-start.16
  670.3 4.5 collective-permute-start.18
  672.3 5.5 collective-permute-start.19
  753.0 5.9 collective-permute-start.21
  756.4 7.9 collective-permute-start.20
  764.3 4.7 collective-permute-start.22
  766.4 5.1 collective-permute-start.23
  907.9 5.9 collective-permute-start.25
  911.3 7.9 collective-permute-start.24
  919.2 4.5 collective-permute-start.26
  921.2 5.1 collective-permute-start.27
  1064.0 6.0 collective-permute-start.29
  1067.4 7.9 collective-permute-start.28
  1075.4 6.3 collective-permute-start.30
  1077.3 5.1 collective-permute-start.31
  1313.8 19.7 %copy-start.2 = (f32[8,16,512]{2,1,0:T(8,128)}, f32[8,16,512]{2,1,0:T(8,128)S(1)}, u32[]{:S(2)}) copy-start(f32[8,16,512]{2,1,0:T(8,128)S(1)} %multiply_add_fusion) | copy-start | bytes 786436
  1313.8 5.9 collective-permute-start.33
  1317.1 7.9 collective-permute-start.32
  1325.1 4.5 collective-permute-start.34
  1327.1 5.5 collective-permute-start.35
